TPU v7x, 128 devices: a whole 4x4x4 slice. The times are simulated.
128 devices in a mesh: gx: 16 (over y, z), gy: 8 (over x, core).
Axes of the slice: x: 4, y: 4, z: 4, core: 2. Of those that a mesh axis runs over, the one named last changes fastest.
Arguments:
- features: bfloat16 [2048, 512, 128], P('gx', 'gy'), may hold values from -6 to 6
- cotangent: bfloat16 [2048, 512, 128], P('gx', 'gy'), may hold values from -31 to 31
- kernel: float32 [7, 7, 128], replicated, may hold values from -0.875 to 0.875
- kernel_bias: float32 [128], replicated, may hold values from -3 to 3
- norm_gain: float32 [128], replicated, may hold values from 0.1 to 1.9
- norm_shift: float32 [128], replicated, may hold values from -3 to 3
- w_up: bfloat16 [128, 512], replicated, may hold values from -0.5 to 0.5
- b_up: float32 [512], replicated, may hold values from -3 to 3
- w_down: bfloat16 [512, 128], replicated, may hold values from -0.25 to 0.25
- b_down: float32 [128], replicated, may hold values from -3 to 3
- layer_scale: float32 [128], replicated, may hold values from 0.3 to 3
Outputs:
- d_features: bfloat16 [2048, 512, 128], P('gx', 'gy')
- d_kernel: float32 [7, 7, 128], replicated
- d_kernel_bias: float32 [128], replicated
- d_norm_gain: float32 [128], replicated
- d_norm_shift: float32 [128], replicated
- d_w_up: float32 [128, 512], replicated
- d_b_up: float32 [512], replicated
- d_w_down: float32 [512, 128], replicated
- d_b_down: float32 [128], replicated
- d_layer_scale: float32 [128], replicated
All inputs are finite; a program needn't handle non-finite values.
Results may differ from a plain program's by a relative error of at most 0.0072.
Values may be sent and summed in bfloat16 or wider, within the bound.
No kernel may reach another device: no remote copies, remote signals or barrier semaphores. Data moves between devices by JAX's collectives and lax.ppermute only.
A program may use at most 64 MiB of HBM per device.

v0:
```python
import math
import jax
import jax.numpy as jnp
from jax import lax
from jax.sharding import PartitionSpec as P

EPSILON = 1e-06


def extended(cells, sides, width):
    for axis, dim in sides:
        count = lax.axis_size(axis)
        head = lax.slice_in_dim(cells, 0, width, axis=dim)
        tail = lax.slice_in_dim(cells, cells.shape[dim] - width, cells.shape[dim], axis=dim)
        cells = jnp.concatenate(
            [
                lax.ppermute(tail, axis, [(i, (i + 1) % count) for i in range(count)]),
                cells,
                lax.ppermute(head, axis, [((i + 1) % count, i) for i in range(count)]),
            ],
            axis=dim,
        )
    return cells


def gelu_pair(hidden):
    erf_part = jax.scipy.special.erf(hidden * 0.7071067811865476)
    value = 0.5 * hidden * (1.0 + erf_part)
    slope_value = (
        0.5 * (1.0 + erf_part) + hidden * jnp.exp(-0.5 * hidden * hidden) * 0.3989422804014327
    )
    return (value, slope_value)


def product(spec, left, right):
    return jnp.einsum(spec, left, right, preferred_element_type=jnp.float32)


def depthwise(padded, kernel, row_count, col_count):
    tap_count = kernel.shape[0]
    accum = jnp.zeros((row_count, col_count, kernel.shape[2]), jnp.float32)
    for row_tap in range(tap_count):
        for col_tap in range(tap_count):
            window = padded[row_tap : row_tap + row_count, col_tap : col_tap + col_count]
            accum = accum + window.astype(jnp.float32) * kernel[row_tap, col_tap]
    return accum


def spread_back(padded, kernel, row_count, col_count):
    tap_count = kernel.shape[0]
    edge_cells = tap_count - 1
    accum = jnp.zeros((row_count, col_count, kernel.shape[2]), jnp.float32)
    for row_tap in range(tap_count):
        for col_tap in range(tap_count):
            window = padded[
                edge_cells - row_tap : edge_cells - row_tap + row_count,
                edge_cells - col_tap : edge_cells - col_tap + col_count,
            ]
            accum = accum + window * kernel[row_tap, col_tap]
    return accum


def kernel_grad(slopes_in, padded, tap_count):
    row_count, col_count = (slopes_in.shape[0], slopes_in.shape[1])
    rows_out = []
    for row_tap in range(tap_count):
        line = []
        for col_tap in range(tap_count):
            window = padded[row_tap : row_tap + row_count, col_tap : col_tap + col_count].astype(
                jnp.float32
            )
            line.append(jnp.sum(slopes_in * window, axis=(0, 1)))
        rows_out.append(jnp.stack(line, 0))
    return jnp.stack(rows_out, 0)


def mask_edges(padded, width):
    col_total = padded.shape[1]
    inner_cols = col_total - 2 * width
    grid_cols = inner_cols * lax.axis_size("gy")
    col_place = lax.axis_index("gy") * inner_cols + lax.iota(jnp.int32, col_total) - width
    keep_mask = (col_place >= 0) & (col_place < grid_cols)
    return jnp.where(keep_mask[None, :, None], padded, jnp.zeros((), padded.dtype))


def layer_back(conv_out, cotan, norm_gain, norm_shift, w_up, b_up, w_down, b_down, layer_scale):
    chan_mean = jnp.mean(conv_out, axis=-1, keepdims=True)
    centred = conv_out - chan_mean
    inv_std = lax.rsqrt(jnp.mean(centred * centred, axis=-1, keepdims=True) + EPSILON)
    normed = centred * inv_std
    normal_out = (normed * norm_gain + norm_shift).astype(jnp.bfloat16)
    hidden = product("rwc,ce->rwe", normal_out, w_up) + b_up
    active, gelu_slope = gelu_pair(hidden)
    active = active.astype(jnp.bfloat16)
    output = product("rwe,ec->rwc", active, w_down) + b_down
    cot_float = cotan.astype(jnp.float32)
    d_output = (cot_float * layer_scale).astype(jnp.bfloat16)
    d_active = product("rwc,ec->rwe", d_output, w_down)
    d_hidden = (d_active * gelu_slope).astype(jnp.bfloat16)
    d_normal = product("rwe,ce->rwc", d_hidden, w_up)
    d_normed = d_normal * norm_gain
    first_mean = jnp.mean(d_normed, axis=-1, keepdims=True)
    second_mean = jnp.mean(d_normed * normed, axis=-1, keepdims=True)
    d_conv = inv_std * (d_normed - first_mean - normed * second_mean)
    d_gain = jnp.sum(d_normal * normed, axis=(0, 1))
    d_shift = jnp.sum(d_normal, axis=(0, 1))
    d_wup = product("rwc,rwe->ce", normal_out, d_hidden)
    d_bup = jnp.sum(d_hidden.astype(jnp.float32), axis=(0, 1))
    d_wdown = product("rwe,rwc->ec", active, d_output)
    d_bdown = jnp.sum(d_output.astype(jnp.float32), axis=(0, 1))
    d_lscale = jnp.sum(cot_float * output, axis=(0, 1))
    return (d_conv, (d_gain, d_shift, d_wup, d_bup, d_wdown, d_bdown, d_lscale))


def local(
    features,
    cotangent,
    kernel,
    kernel_bias,
    norm_gain,
    norm_shift,
    w_up,
    b_up,
    w_down,
    b_down,
    layer_scale,
):
    tap_count = kernel.shape[0]
    reach_cells = tap_count // 2
    row_count, col_count = (features.shape[0], features.shape[1])
    padded_x = mask_edges(extended(features, (("gx", 0), ("gy", 1)), reach_cells), reach_cells)
    conv_out = depthwise(padded_x, kernel, row_count, col_count) + kernel_bias
    d_conv, layer_grads = layer_back(
        conv_out, cotangent, norm_gain, norm_shift, w_up, b_up, w_down, b_down, layer_scale
    )
    d_kern = kernel_grad(d_conv, padded_x, tap_count)
    d_kbias = jnp.sum(d_conv, axis=(0, 1))
    padded_slope = mask_edges(extended(d_conv, (("gx", 0), ("gy", 1)), reach_cells), reach_cells)
    spread = spread_back(padded_slope, kernel, row_count, col_count)
    d_features = (cotangent.astype(jnp.float32) + spread).astype(jnp.bfloat16)
    d_gain, d_shift, d_wup, d_bup, d_wdown, d_bdown, d_lscale = layer_grads
    summed = lax.psum(
        (d_kern, d_kbias, d_gain, d_shift, d_wup, d_bup, d_wdown, d_bdown, d_lscale), ("gx", "gy")
    )
    factor = 1.0 / math.sqrt(row_count * col_count * lax.axis_size("gx") * lax.axis_size("gy"))
    return (d_features,) + tuple((entry * factor for entry in summed))


def solution(mesh):
    placed = (P("gx", "gy", None), P("gx", "gy", None), P(), P(), P(), P(), P(), P(), P(), P(), P())
    return jax.shard_map(
        local,
        mesh=mesh,
        in_specs=placed,
        out_specs=(P("gx", "gy", None), P(), P(), P(), P(), P(), P(), P(), P(), P()),
        check_vma=False,
    )
```

profile of v0, /device:TPU:1, one launch (start us, length us, event | category | flops | bytes accessed | tf_op | source)
XLA Modules:
  0.0 487.0 jit_solution(8291468814353680774)
XLA Ops:
  7.2 0.0 copy-start
  7.2 0.0 all-reduce.4.cloned.1.call-start
  7.3 0.0 copy-start.3
  7.3 3.1 copy.22
  10.4 0.1 fusion.166
  10.4 2.5 collective-permute-start
  13.0 4.9 %collective-permute-start.1 = (bf16[3,64,128]{2,0,1:T(4,128)(2,1)S(1)}, bf16[3,64,128]{2,0,1:T(4,128)(2,1)S(1)}, u32[]{:S(2)}, u32[]{:S(2)}) collective-permute-start(bf16[3,64,128]{2,0,1:T(4,128)(2,1)S(1)} %get-tuple-element.93), channel_id=1, source_target_pairs={{8,0},{16,8},{24,16},{32,24},{40,32},{48,40},{56,48},{64,56},{72,6... | collective-permute-start | bytes 147464 | tf_op jit(solution)/shard_map/ppermute | solution.py:19
  18.0 1.1 convert_reduce_fusion.1
  19.1 0.1 collective-permute-done
  19.2 0.1 collective-permute-done.1
  19.2 0.1 pad_maximum_fusion.5
  19.3 2.6 collective-permute-start.2
  21.9 1.7 collective-permute-done.2
  23.6 2.4 collective-permute-done.3
  26.0 2.9 maximum_select_fusion.1
  29.0 33.0 %fusion.163 = (f32[128,64]{0,1:T(8,128)S(1)}, f32[128,64,128]{2,0,1:T(8,128)S(1)}) fusion(f32[128]{0:T(128)S(1)} %copy-done.11, f32[128]{0:T(128)S(1)} %get-tuple-element.141, bf16[134,70,128]{2,0,1:T(8,128)(2,1)S(1)} %maximum_select_fusion.1, f32[128]{0:T(128)S(1)} %get-tuple-element.142, f32[128]{0:T(128)S(1)} %get-tuple-element.95, ...), kind=kLoop, calls=%fused_computation.403 | loop fusion | flops 155181056 | bytes 107013120 | tf_op jit(solution)/shard_map/reduce_sum | solution.py:87
  62.0 0.0 copy-start.8
  62.0 0.0 copy-start.9
  62.0 2.7 multiply_reduce_fusion.2
  64.8 8.6 %multiply_convert_fusion = (bf16[128,64,512]{2,0,1:T(8,128)(2,1)}, f32[128,64,512]{2,0,1:T(8,128)S(1)}) fusion(f32[512]{0:T(512)S(1)} %copy-done.9, bf16[128,512]{1,0:T(8,128)(2,1)S(1)} %copy-done, f32[128,64,128]{2,0,1:T(8,128)S(1)} %get-tuple-element.85, f32[128]{0:T(128)S(1)} %copy-done.8, f32[128]{0:T(128)S(1)} %copy-done.7, ...), kind=kOutput, calls=%fused_computation.7 | convolution fusion | flops 1104150528 | bytes 29559808 | tf_op jit(solution)/shard_map/rwc,ce->rwe/dot_general | solution.py:36
  73.5 10.9 %convert_reduce_fusion = (f32[512]{0:T(512)S(1)}, bf16[128,64,512]{2,0,1:T(8,128)(2,1)S(1)}) fusion(f32[128,64,512]{2,0,1:T(8,128)S(1)} %get-tuple-element.147, f32[512]{0:T(512)S(1)} %copy-done.9, bf16[512,128]{1,0:T(8,128)(2,1)S(1)} %copy-done.12, f32[128]{0:T(128)S(1)} %copy-done.10, bf16[128,64,128]{2,1,0:T(8,128)(2,1)S(1)} %copy-done.4), kind=kOutput, calls=%fused_computation.8 | convolution fusion | flops 1131412992 | bytes 27398656 | tf_op jit(solution)/shard_map/rwc,ec->rwe/dot_general | solution.py:36
  84.4 4.2 convolution_bitcast_fusion.1
  88.6 4.8 multiply_reduce_fusion
  93.3 13.4 %fusion.102 = (f32[128]{0:T(128)S(1)}, f32[128]{0:T(128)S(1)}, f32[128]{0:T(128)S(1)}, f32[128]{0:T(128)S(1)}, f32[128]{0:T(128)S(1)}, /*index=5*/f32[128]{0:T(1...) fusion(bf16[134,70,128]{2,0,1:T(8,128)(2,1)S(1)} %maximum_selec, ...), kind=kLoop, calls=%fused_computation.208 | loop fusion | flops 63960832 | bytes 50472448 | tf_op jit(solution)/shard_map/reduce_sum | solution.py:72
  106.8 11.0 %fusion.84 = (f32[128]{0:T(128)S(1)}, f32[128]{0:T(128)S(1)}, f32[128]{0:T(128)S(1)}, f32[128]{0:T(128)S(1)}, f32[128]{0:T(128)S(1)}, /*index=5*/f32[128]{0:T(12...) fusion(f32[128,64,128]{2,0,1:T(8,128)S(1)} %get-tuple-element.8, ...), kind=kLoop, calls=%fused_computation.190 | loop fusion | flops 56620800 | bytes 41952256 | tf_op jit(solution)/shard_map/reduce_sum | solution.py:72
  117.8 8.2 %fusion.43 = (f32[128]{0:T(128)S(1)}, f32[128]{0:T(128)S(1)}, f32[128]{0:T(128)S(1)}, f32[128]{0:T(128)S(1)}, f32[128]{0:T(128)S(1)}, /*index=5*/f32[128]{0:T(12...) fusion(f32[128,64,128]{2,0,1:T(8,128)S(1)} %get-tuple-element.8, ...), kind=kLoop, calls=%fused_computation.149 | loop fusion | flops 41941248 | bytes 31464448 | tf_op jit(solution)/shard_map/reduce_sum | solution.py:72
  126.2 4.3 convolution_bitcast_fusion
  130.5 6.2 %fusion.105 = f32[128]{0:T(128)S(1)} fusion(bf16[128,64,512]{2,0,1:T(8,128)(2,1)} %get-tuple-element.146, f32[128]{0:T(128)S(1)} %copy-done.13, bf16[128,64,128]{2,1,0:T(8,128)(2,1)S(1)} %copy-done.5, bf16[512,128]{1,0:T(8,128)(2,1)S(1)} %copy-done.12), kind=kOutput, calls=%fused_computation.211 | convolution fusion | flops 1077936000 | bytes 10617856 | tf_op jit(solution)/shard_map/rwe,ec->rwc/dot_general | solution.py:36
  137.0 67.9 %all-reduce = (f32[7,7,128]{2,1,0:T(8,128)S(1)}, f32[128]{0:T(128)S(1)}, f32[128]{0:T(128)S(1)}, f32[128]{0:T(128)S(1)}, f32[512]{0:T(512)S(1)}, /*index=5*/f32[128]{0:T(128)S(1)}, f32[128]{0:T(128)S(1)}) all-reduce(f32[7,7,128]{2,1,0:T(8,128)S(1)} %constant_dynamic-update-slice_fusion, ...), channel_id=1, replica_groups=mesh['gx'=16,'gy'=8] {'gx','gy'}, use_global_device_ids=true, to_apply=%region_53.54 | all-reduce | flops 7424 | bytes 59392 | tf_op jit(solution)/shard_map/psum | solution.py:142
  204.9 0.6 broadcast_multiply_fusion.5
  205.6 0.6 broadcast_multiply_fusion.6
  206.1 0.5 broadcast_multiply_fusion.10
  206.6 0.5 broadcast_multiply_fusion.11
  207.2 0.5 broadcast_multiply_fusion.7
  207.7 0.5 broadcast_multiply_fusion.8
  208.2 4.8 collective-permute-start.5
  213.0 0.0 all-reduce.4.cloned.1.call-update
  213.0 0.5 broadcast_multiply_fusion.9
  213.5 1.8 collective-permute-done.4
  215.3 1.1 pad_maximum_fusion.2
  216.4 1.5 collective-permute-start.6
  217.9 0.8 collective-permute-start.7
  218.8 136.7 %all-reduce.4.cloned.1.call-done = (f32[128,512]{1,0:T(8,128)}, f32[512,128]{1,0:T(8,128)}) async-done(((f32[128,512]{1,0:T(8,128)}, f32[512,128]{1,0:T(8,128)}), (f32[128,512]{1,0:T(8,128)}, f32[512,128]{1,0:T(8,128)})) %all-reduce.4.cloned.1.call-update) | async-done | bytes 524304 | tf_op jit(solution)/shard_map/psum | solution.py:142
  355.4 1.7 broadcast_multiply_fusion
  357.1 1.7 broadcast_multiply_fusion.1
  358.8 5.5 %maximum_select_fusion = f32[134,70,128]{2,0,1:T(8,128)} fusion(f32[134,3,128]{2,0,1:T(8,128)S(1)} %collective-permute-done.7, f32[3,64,128]{2,0,1:T(4,128)S(1)} %collective-permute-done.5, f32[128,64,128]{2,0,1:T(8,128)} %copy-done.2, f32[3,64,128]{2,0,1:T(4,128)S(1)} %collective-permute-done.4, f32[134,3,128]{2,0,1:T(8,128)S(1)} %collective-permute-done.6, ...), kind=kLoop, calls=%fused_computation.111 | loop fusion | flops 6003200 | bytes 9605190 | tf_op jit(solution)/shard_map/jit(_where)/select_n | solution.py:83
  364.3 111.4 %fusion.104 = bf16[128,64,128]{2,0,1:T(8,128)(2,1)} fusion(f32[134,70,128]{2,0,1:T(8,128)} %maximum_select_fusion, f32[128]{0:T(128)S(1)} %get-tuple-element.141, f32[128]{0:T(128)S(1)} %get-tuple-element.142, f32[128]{0:T(128)S(1)} %get-tuple-element.95, f32[128]{0:T(128)S(1)} %get-tuple-element.96, f32[128]{0:T(128)S(1)} %get-tuple-element.97, ...), kind=kLoop, calls=%fused_computation.210 | loop fusion | flops 104857600 | bytes 209740288 | tf_op jit(solution)/shard_map/convert_element_type | solution.py:140
  475.7 4.3 copy.27
  (56 shorter events, 0.4 us)
Async XLA Ops:
  7.2 57.6 %copy-start = (bf16[128,512]{1,0:T(8,128)(2,1)S(1)}, bf16[128,512]{1,0:T(8,128)(2,1)}, u32[]{:S(2)}) copy-start(bf16[128,512]{1,0:T(8,128)(2,1)} %param.17) | copy-start | bytes 393220
  7.2 10.7 %copy-start.6 = (f32[7,7,128]{2,1,0:T(8,128)S(1)}, f32[7,7,128]{2,1,0:T(8,128)}, u32[]{:S(2)}) copy-start(f32[7,7,128]{2,1,0:T(8,128)} %param.13) | copy-start | bytes 75268
  7.2 10.7 %copy-start.10 = (f32[128]{0:T(128)S(1)}, f32[128]{0:T(128)}, u32[]{:S(2)}) copy-start(f32[128]{0:T(128)} %param.21) | copy-start | bytes 1540
  7.2 348.2 %all-reduce.4.cloned.1.call-start = ((), (), s32[]{:S(2)}) async-start(), calls=%async_computation | async-start | bytes 1048576 | tf_op jit(solution)/shard_map/psum | solution.py:142
  7.3 10.7 %copy-start.3 = (bf16[128,64,128]{2,1,0:T(8,128)(2,1)S(1)}, bf16[128,64,128]{2,1,0:T(8,128)(2,1)}, u32[]{:S(2)}) copy-start(bf16[128,64,128]{2,1,0:T(8,128)(2,1)} %param.12) | copy-start | bytes 6291460
  10.4 8.8 %collective-permute-start = (bf16[3,64,128]{2,0,1:T(4,128)(2,1)S(1)}, bf16[3,64,128]{2,0,1:T(4,128)(2,1)S(1)}, u32[]{:S(2)}, u32[]{:S(2)}) collective-permute-start(bf16[3,64,128]{2,0,1:T(4,128)(2,1)S(1)} %get-tuple-element.92), channel_id=1, source_target_pairs={{0,8},{8,16},{16,24},{24,32},{32,40},{40,48},{48,56},{56,64},{64,7... | collective-permute-start | bytes 147464 | tf_op jit(solution)/shard_map/ppermute | solution.py:17
  13.0 6.3 %collective-permute-start.1 = (bf16[3,64,128]{2,0,1:T(4,128)(2,1)S(1)}, bf16[3,64,128]{2,0,1:T(4,128)(2,1)S(1)}, u32[]{:S(2)}, u32[]{:S(2)}) collective-permute-start(bf16[3,64,128]{2,0,1:T(4,128)(2,1)S(1)} %get-tuple-element.93), channel_id=1, source_target_pairs={{8,0},{16,8},{24,16},{32,24},{40,32},{48,40},{56,48},{64,56},{72,6... | collective-permute-start | bytes 147464 | tf_op jit(solution)/shard_map/ppermute | solution.py:19
  19.1 9.9 %copy-start.11 = (f32[128]{0:T(128)S(1)}, f32[128]{0:T(128)}, u32[]{:S(2)}) copy-start(f32[128]{0:T(128)} %param.14) | copy-start | bytes 1540
  19.3 4.3 collective-permute-start.2
  21.9 4.1 collective-permute-start.3
  62.0 2.8 copy-start.7
  62.0 2.8 copy-start.8
  62.0 2.8 copy-start.9
  64.8 8.7 %copy-start.4 = (bf16[128,64,128]{2,1,0:T(8,128)(2,1)S(1)}, bf16[128,64,128]{2,1,0:T(8,128)(2,1)}, u32[]{:S(2)}) copy-start(bf16[128,64,128]{2,1,0:T(8,128)(2,1)} %param.12) | copy-start | bytes 6291460
  64.8 8.6 %copy-start.12 = (bf16[512,128]{1,0:T(8,128)(2,1)S(1)}, bf16[512,128]{1,0:T(8,128)(2,1)}, u32[]{:S(2)}) copy-start(bf16[512,128]{1,0:T(8,128)(2,1)} %param.19) | copy-start | bytes 393220
  93.3 32.8 %slice-start = ((s8[8388608]{0:T(1024)(128)(4,1)}), s8[4194304]{0:T(1024)(128)(4,1)S(1)}, s32[]{:S(2)}) async-start(s8[8388608]{0:T(1024)(128)(4,1)} %bitcast.185), calls=%async_computation.1 | async-start | bytes 8388608
  106.7 19.3 %copy-start.2 = (f32[128,64,128]{2,0,1:T(8,128)}, f32[128,64,128]{2,0,1:T(8,128)S(1)}, u32[]{:S(2)}) copy-start(f32[128,64,128]{2,0,1:T(8,128)S(1)} %get-tuple-element.83) | copy-start | bytes 12582916
  106.8 19.4 %slice-start.1 = ((s8[8388608]{0:T(1024)(128)(4,1)}), s8[4194304]{0:T(1024)(128)(4,1)S(1)}, s32[]{:S(2)}) async-start(s8[8388608]{0:T(1024)(128)(4,1)} %bitcast.185), calls=%async_computation.2 | async-start | bytes 8388608
  117.8 8.3 %copy-start.5 = (bf16[128,64,128]{2,1,0:T(8,128)(2,1)S(1)}, bf16[128,64,128]{2,1,0:T(8,128)(2,1)}, u32[]{:S(2)}) copy-start(bf16[128,64,128]{2,1,0:T(8,128)(2,1)} %param.12) | copy-start | bytes 6291460
  126.2 4.4 copy-start.13
  208.2 7.1 %collective-permute-start.4 = (f32[3,64,128]{2,0,1:T(4,128)S(1)}, f32[3,64,128]{2,0,1:T(4,128)S(1)}, u32[]{:S(2)}, u32[]{:S(2)}) collective-permute-start(f32[3,64,128]{2,0,1:T(4,128)S(1)} %get-tuple-element.88), channel_id=1, source_target_pairs={{0,8},{8,16},{16,24},{24,32},{32,40},{40,48},{48,56},{56,64},{64,7... | collective-permute-start | bytes 294920 | tf_op jit(solution)/shard_map/ppermute | solution.py:17
  208.2 7.1 %collective-permute-start.5 = (f32[3,64,128]{2,0,1:T(4,128)S(1)}, f32[3,64,128]{2,0,1:T(4,128)S(1)}, u32[]{:S(2)}, u32[]{:S(2)}) collective-permute-start(f32[3,64,128]{2,0,1:T(4,128)S(1)} %get-tuple-element.89), channel_id=1, source_target_pairs={{8,0},{16,8},{24,16},{32,24},{40,32},{48,40},{56,48},{64,56},{72,6... | collective-permute-start | bytes 294920 | tf_op jit(solution)/shard_map/ppermute | solution.py:19
  216.4 142.4 %collective-permute-start.6 = (f32[134,3,128]{2,0,1:T(8,128)S(1)}, f32[134,3,128]{2,0,1:T(8,128)S(1)}, u32[]{:S(2)}, u32[]{:S(2)}) collective-permute-start(f32[134,3,128]{2,0,1:T(8,128)S(1)} %get-tuple-element.86), channel_id=1, source_target_pairs={{0,1},{1,2},{2,3},{3,4},{4,5},{5,6},{6,7},{7,0},{8,9},{9,10},{10,1... | collective-permute-start | bytes 617480 | tf_op jit(solution)/shard_map/ppermute | solution.py:17
  217.9 140.9 %collective-permute-start.7 = (f32[134,3,128]{2,0,1:T(8,128)S(1)}, f32[134,3,128]{2,0,1:T(8,128)S(1)}, u32[]{:S(2)}, u32[]{:S(2)}) collective-permute-start(f32[134,3,128]{2,0,1:T(8,128)S(1)} %get-tuple-element.87), channel_id=1, source_target_pairs={{1,0},{2,1},{3,2},{4,3},{5,4},{6,5},{7,6},{0,7},{9,8},{10,9},{11,1... | collective-permute-start | bytes 617480 | tf_op jit(solution)/shard_map/ppermute | solution.py:19
  364.3 115.7 %copy-start.1 = (bf16[128,512]{1,0:T(8,128)(2,1)S(1)}, bf16[128,512]{1,0:T(8,128)(2,1)}, u32[]{:S(2)}) copy-start(bf16[128,512]{1,0:T(8,128)(2,1)} %param.17) | copy-start | bytes 393220
Sparse Core Ops, SparseCore 0:
  213.1 142.2 all-reduce.3
where the time goes:
time: 490 us; the launch traced here: 487 us
  other arithmetic  198 us (40%)
  waiting for transfers between devices  143 us (29%)
  blocking collectives  67.9 us (14%)
  matrix products  39 us (8%)
  starting transfers between devices  17.3 us (4%)
  between operations  14.7 us (3%)
  local copies, waits for them, and re-layouts  7.79 us (2%)
    psum x1, waiting for transfers between devices, local(): lax.psum((d_kern, d_kbias, d_gain, d_shift, d_wup, d_bup, d_wdown, d_bdow...  137 us
    convert_element_type x1, other arithmetic, local(): d_features = (cotangent.astype(jnp.float32) + spread).astype(jnp.bfloat16)  111 us
    psum x1, blocking collectives, local(): lax.psum((d_kern, d_kbias, d_gain, d_shift, d_wup, d_bup, d_wdown, d_bdow...  67.9 us
    dot_general x6, matrix products, product(): return jnp.einsum(spec, left, right, preferred_element_type=jnp.float32)  39 us
    reduce_sum x1, other arithmetic, layer_back(): chan_mean = jnp.mean(conv_out, axis=-1, keepdims=True)  33 us
    reduce_sum x3, other arithmetic, kernel_grad(): line.append(jnp.sum(slopes_in * window, axis=(0, 1)))  32.6 us
    ppermute x4, starting transfers between devices, extended(): lax.ppermute(head, axis, [((i + 1) % count, i) for i in range(count)])  10.6 us
  transfers between devices with their start and end apart: 9, of which 5 were waited for; matrix products, arithmetic and copies ran while one was open for 1% of the time, Pallas kernels for 0%

commit v1 on v0

--- a/solution.py
+++ b/solution.py
@@ -140,7 +140,11 @@
     d_features = (cotangent.astype(jnp.float32) + spread).astype(jnp.bfloat16)
     d_gain, d_shift, d_wup, d_bup, d_wdown, d_bdown, d_lscale = layer_grads
     summed = lax.psum(
-        (d_kern, d_kbias, d_gain, d_shift, d_wup, d_bup, d_wdown, d_bdown, d_lscale), ("gx", "gy")
+        lax.psum(
+            (d_kern, d_kbias, d_gain, d_shift, d_wup, d_bup, d_wdown, d_bdown, d_lscale),
+            axis_name="gy",
+        ),
+        axis_name="gx",
     )
     factor = 1.0 / math.sqrt(row_count * col_count * lax.axis_size("gx") * lax.axis_size("gy"))
     return (d_features,) + tuple((entry * factor for entry in summed))

time: 490 us -> 435 us (0.89)
  waiting for transfers between devices: 143 us -> 53.9 us
  blocking collectives: 67.9 us -> 84.7 us
  starting transfers between devices: 17.3 us -> 33.5 us
    psum x1, waiting for transfers between devices: 137 us -> 47.8 us  [local(): lax.psum((d_kern, d_kbias, d_gain, d_shift, d_wup, d_bup, d_wdown, d_bdow...]
    psum x0 -> x1, blocking collectives: none -> 61.3 us  [local(): lax.psum(lax.psum((d_kern, d_kbias, d_gain, d_shift, d_wup, d_bup, d_wdow...]
    psum x1, blocking collectives: 67.9 us -> 23.4 us  [local(): lax.psum((d_kern, d_kbias, d_gain, d_shift, d_wup, d_bup, d_wdown, d_bdow...]
    ppermute x4, starting transfers between devices: 6.71 us -> 21.8 us  [extended(): lax.ppermute(tail, axis, [(i, (i + 1) % count) for i in range(count)])]
  transfers between devices with their start and end apart: 9 -> 10, of which waited for: 5 -> 5; matrix products, arithmetic and copies ran while one was open for 1% -> 29% of each run, Pallas kernels for 0% -> 0%
where the time goes in v1:
time: 435 us; the launch traced here: 431 us
  other arithmetic  198 us (46%)
  blocking collectives  84.7 us (19%)
  waiting for transfers between devices  53.9 us (12%)
  matrix products  39 us (9%)
  starting transfers between devices  33.5 us (8%)
  between operations  14.7 us (3%)
  local copies, waits for them, and re-layouts  7.79 us (2%)
    convert_element_type x1, other arithmetic, local(): d_features = (cotangent.astype(jnp.float32) + spread).astype(jnp.bfloat16)  111 us
    psum x1, blocking collectives, local(): lax.psum(lax.psum((d_kern, d_kbias, d_gain, d_shift, d_wup, d_bup, d_wdow...  61.3 us
    psum x1, waiting for transfers between devices, local(): lax.psum((d_kern, d_kbias, d_gain, d_shift, d_wup, d_bup, d_wdown, d_bdow...  47.8 us
    dot_general x6, matrix products, product(): return jnp.einsum(spec, left, right, preferred_element_type=jnp.float32)  39 us
    reduce_sum x1, other arithmetic, layer_back(): chan_mean = jnp.mean(conv_out, axis=-1, keepdims=True)  33 us
    reduce_sum x3, other arithmetic, kernel_grad(): line.append(jnp.sum(slopes_in * window, axis=(0, 1)))  32.6 us
    psum x1, blocking collectives, local(): lax.psum((d_kern, d_kbias, d_gain, d_shift, d_wup, d_bup, d_wdown, d_bdow...  23.4 us
    ppermute x4, starting transfers between devices, extended(): lax.ppermute(tail, axis, [(i, (i + 1) % count) for i in range(count)])  21.8 us
  transfers between devices with their start and end apart: 10, of which 5 were waited for; matrix products, arithmetic and copies ran while one was open for 29% of the time, Pallas kernels for 0%

profile of v1, /device:TPU:1, one launch (start us, length us, event | category | flops | bytes accessed | tf_op | source)
XLA Modules:
  0.0 431.1 jit_solution(16451334733335710789)
XLA Ops:
  7.2 0.0 copy-start
  7.2 0.0 all-reduce.9.cloned.1.call-start
  7.3 3.1 copy.22
  10.4 0.1 fusion.166
  10.4 2.5 collective-permute-start
  13.0 4.9 %collective-permute-start.1 = (bf16[3,64,128]{2,0,1:T(4,128)(2,1)S(1)}, bf16[3,64,128]{2,0,1:T(4,128)(2,1)S(1)}, u32[]{:S(2)}, u32[]{:S(2)}) collective-permute-start(bf16[3,64,128]{2,0,1:T(4,128)(2,1)S(1)} %get-tuple-element.102), channel_id=1, source_target_pairs={{8,0},{16,8},{24,16},{32,24},{40,32},{48,40},{56,48},{64,56},{72,6... | collective-permute-start | bytes 147464 | tf_op jit(solution)/shard_map/ppermute | solution.py:19
  18.0 1.1 convert_reduce_fusion.1
  19.1 0.1 collective-permute-done
  19.2 0.1 collective-permute-done.1
  19.2 0.1 pad_maximum_fusion.5
  19.3 2.6 collective-permute-start.2
  21.9 1.7 collective-permute-done.2
  23.6 2.4 collective-permute-done.3
  26.0 2.9 maximum_select_fusion.1
  29.0 33.0 %fusion.163 = (f32[128,64]{0,1:T(8,128)S(1)}, f32[128,64,128]{2,0,1:T(8,128)S(1)}) fusion(f32[128]{0:T(128)S(1)} %copy-done.11, f32[128]{0:T(128)S(1)} %get-tuple-element.150, bf16[134,70,128]{2,0,1:T(8,128)(2,1)S(1)} %maximum_select_fusion.1, f32[128]{0:T(128)S(1)} %get-tuple-element.151, f32[128]{0:T(128)S(1)} %get-tuple-element.104, ...), kind=kLoop, calls=%fused_computation.403 | loop fusion | flops 155181056 | bytes 107013120 | tf_op jit(solution)/shard_map/reduce_sum | solution.py:87
  62.0 2.7 multiply_reduce_fusion.2
  64.8 8.6 %multiply_convert_fusion = (bf16[128,64,512]{2,0,1:T(8,128)(2,1)}, f32[128,64,512]{2,0,1:T(8,128)S(1)}) fusion(f32[512]{0:T(512)S(1)} %copy-done.9, bf16[128,512]{1,0:T(8,128)(2,1)S(1)} %copy-done, f32[128,64,128]{2,0,1:T(8,128)S(1)} %get-tuple-element.94, f32[128]{0:T(128)S(1)} %copy-done.8, f32[128]{0:T(128)S(1)} %copy-done.7, ...), kind=kOutput, calls=%fused_computation.7 | convolution fusion | flops 1104150528 | bytes 29559808 | tf_op jit(solution)/shard_map/rwc,ce->rwe/dot_general | solution.py:36
  73.5 10.9 %convert_reduce_fusion = (f32[512]{0:T(512)S(1)}, bf16[128,64,512]{2,0,1:T(8,128)(2,1)S(1)}) fusion(f32[128,64,512]{2,0,1:T(8,128)S(1)} %get-tuple-element.156, f32[512]{0:T(512)S(1)} %copy-done.9, bf16[512,128]{1,0:T(8,128)(2,1)S(1)} %copy-done.12, f32[128]{0:T(128)S(1)} %copy-done.10, bf16[128,64,128]{2,1,0:T(8,128)(2,1)S(1)} %copy-done.4), kind=kOutput, calls=%fused_computation.8 | convolution fusion | flops 1131412992 | bytes 27398656 | tf_op jit(solution)/shard_map/rwc,ec->rwe/dot_general | solution.py:36
  84.4 4.2 convolution_bitcast_fusion.1
  88.6 4.8 %multiply_reduce_fusion = (f32[128]{0:T(128)S(1)}, f32[128,64]{0,1:T(8,128)S(1)}, f32[128,64]{0,1:T(8,128)S(1)}, f32[128]{0:T(128)S(1)}, f32[128,64,128]{2,0,1:T(8,128)S(1)}) fusion(f32[128,64,128]{2,0,1:T(8,128)S(1)} %get-tuple-element.94, f32[128,64]{0,1:T(8,128)S(1)} %add_rsqrt_fusion, f32[128,64]{0,1:T(8,128)S(1)} %broadcast_multiply_fusion.4, ...), kind=kOutput, calls=%fused_computation.310 | convolution fusion | flops 1083162368 | bytes 17040896 | tf_op jit(solution)/shard_map/rwe,ce->rwc/dot_general | solution.py:36
  93.3 13.4 %fusion.102 = (f32[128]{0:T(128)S(1)}, f32[128]{0:T(128)S(1)}, f32[128]{0:T(128)S(1)}, f32[128]{0:T(128)S(1)}, f32[128]{0:T(128)S(1)}, /*index=5*/f32[128]{0:T(1...) fusion(bf16[134,70,128]{2,0,1:T(8,128)(2,1)S(1)} %maximum_selec, ...), kind=kLoop, calls=%fused_computation.208 | loop fusion | flops 63960832 | bytes 50472448 | tf_op jit(solution)/shard_map/reduce_sum | solution.py:72
  106.8 11.0 %fusion.84 = (f32[128]{0:T(128)S(1)}, f32[128]{0:T(128)S(1)}, f32[128]{0:T(128)S(1)}, f32[128]{0:T(128)S(1)}, f32[128]{0:T(128)S(1)}, /*index=5*/f32[128]{0:T(12...) fusion(f32[128,64,128]{2,0,1:T(8,128)S(1)} %get-tuple-element.9, ...), kind=kLoop, calls=%fused_computation.190 | loop fusion | flops 56620800 | bytes 41952256 | tf_op jit(solution)/shard_map/reduce_sum | solution.py:72
  117.8 8.2 %fusion.43 = (f32[128]{0:T(128)S(1)}, f32[128]{0:T(128)S(1)}, f32[128]{0:T(128)S(1)}, f32[128]{0:T(128)S(1)}, f32[128]{0:T(128)S(1)}, /*index=5*/f32[128]{0:T(12...) fusion(f32[128,64,128]{2,0,1:T(8,128)S(1)} %get-tuple-element.9, ...), kind=kLoop, calls=%fused_computation.149 | loop fusion | flops 41941248 | bytes 31464448 | tf_op jit(solution)/shard_map/reduce_sum | solution.py:72
  126.2 4.3 %convolution_bitcast_fusion = f32[512,128]{1,0:T(8,128)} fusion(bf16[128,64,512]{2,0,1:T(8,128)(2,1)S(1)} %bitcast.186, f32[128]{0:T(128)S(1)} %copy-done.10, bf16[128,64,128]{2,1,0:T(8,128)(2,1)S(1)} %copy-done.5), kind=kOutput, calls=%fused_computation.319 | convolution fusion | flops 1076887552 | bytes 10748416 | tf_op jit(solution)/shard_map/rwe,rwc->ec/dot_general | solution.py:36
  130.5 6.2 %fusion.105 = f32[128]{0:T(128)S(1)} fusion(bf16[128,64,512]{2,0,1:T(8,128)(2,1)} %get-tuple-element.155, f32[128]{0:T(128)S(1)} %copy-done.13, bf16[128,64,128]{2,1,0:T(8,128)(2,1)S(1)} %copy-done.5, bf16[512,128]{1,0:T(8,128)(2,1)S(1)} %copy-done.12), kind=kOutput, calls=%fused_computation.211 | convolution fusion | flops 1077936000 | bytes 10617856 | tf_op jit(solution)/shard_map/rwe,ec->rwc/dot_general | solution.py:36
  137.0 23.4 %all-reduce.2 = (f32[7,7,128]{2,1,0:T(8,128)S(1)}, f32[128]{0:T(128)S(1)}, f32[128]{0:T(128)S(1)}, f32[128]{0:T(128)S(1)}, f32[512]{0:T(512)S(1)}, /*index=5*/f32[128]{0:T(128)S(1)}, f32[128]{0:T(128)S(1)}) all-reduce(f32[7,7,128]{2,1,0:T(8,128)S(1)} %constant_dynamic-update-slice_fusion, ...), channel_id=1, replica_groups=mesh['gx'=16,'gy'=8] {'gy'}, use_global_device_ids=true, to_apply=%region_53.54 | all-reduce | flops 7424 | bytes 59392 | tf_op jit(solution)/shard_map/psum | solution.py:143
  160.3 61.3 %all-reduce = (f32[7,7,128]{2,1,0:T(8,128)S(1)}, f32[128]{0:T(128)S(1)}, f32[128]{0:T(128)S(1)}, f32[128]{0:T(128)S(1)}, f32[512]{0:T(512)S(1)}, /*index=5*/f32[128]{0:T(128)S(1)}, f32[128]{0:T(128)S(1)}) all-reduce(f32[7,7,128]{2,1,0:T(8,128)S(1)} %get-tuple-element.83, ...), channel_id=1, replica_groups=mesh['gx'=16,'gy'=8] {'gx'}, use_global_device_ids=true, to_apply=%region_54.55 | all-reduce | flops 7424 | bytes 59392 | tf_op jit(solution)/shard_map/psum | solution.py:142
  221.7 0.6 broadcast_multiply_fusion.5
  222.3 0.6 broadcast_multiply_fusion.6
  222.8 0.5 broadcast_multiply_fusion.10
  223.4 0.5 broadcast_multiply_fusion.11
  223.9 0.5 broadcast_multiply_fusion.7
  224.4 4.8 %collective-permute-start.5 = (f32[3,64,128]{2,0,1:T(4,128)S(1)}, f32[3,64,128]{2,0,1:T(4,128)S(1)}, u32[]{:S(2)}, u32[]{:S(2)}) collective-permute-start(f32[3,64,128]{2,0,1:T(4,128)S(1)} %get-tuple-element.98), channel_id=1, source_target_pairs={{8,0},{16,8},{24,16},{32,24},{40,32},{48,40},{56,48},{64,56},{72,6... | collective-permute-start | bytes 294920 | tf_op jit(solution)/shard_map/ppermute | solution.py:19
  229.2 0.5 broadcast_multiply_fusion.8
  229.7 0.0 all-reduce.9.cloned.1.call-update
  229.7 0.0 all-reduce.7.cloned.1.call-start
  229.8 1.8 collective-permute-done.4
  231.6 1.1 pad_maximum_fusion.2
  232.6 16.7 %collective-permute-start.6 = (f32[134,3,128]{2,0,1:T(8,128)S(1)}, f32[134,3,128]{2,0,1:T(8,128)S(1)}, u32[]{:S(2)}, u32[]{:S(2)}) collective-permute-start(f32[134,3,128]{2,0,1:T(8,128)S(1)} %get-tuple-element.95), channel_id=1, source_target_pairs={{0,1},{1,2},{2,3},{3,4},{4,5},{5,6},{6,7},{7,0},{8,9},{9,10},{10,1... | collective-permute-start | bytes 617480 | tf_op jit(solution)/shard_map/ppermute | solution.py:17
  249.3 1.9 collective-permute-start.7
  251.2 0.5 broadcast_multiply_fusion.9
  251.7 47.8 %all-reduce.9.cloned.1.call-done = (f32[128,512]{1,0:T(8,128)}, f32[512,128]{1,0:T(8,128)}) async-done(((f32[128,512]{1,0:T(8,128)}, f32[512,128]{1,0:T(8,128)}), (f32[128,512]{1,0:T(8,128)}, f32[512,128]{1,0:T(8,128)})) %all-reduce.9.cloned.1.call-update) | async-done | bytes 524304 | tf_op jit(solution)/shard_map/psum | solution.py:143
  299.5 0.0 all-reduce.7.cloned.1.call-update
  299.6 5.5 %maximum_select_fusion = f32[134,70,128]{2,0,1:T(8,128)} fusion(f32[134,3,128]{2,0,1:T(8,128)S(1)} %collective-permute-done.7, f32[3,64,128]{2,0,1:T(4,128)S(1)} %collective-permute-done.5, f32[128,64,128]{2,0,1:T(8,128)} %copy-done.2, f32[3,64,128]{2,0,1:T(4,128)S(1)} %collective-permute-done.4, f32[134,3,128]{2,0,1:T(8,128)S(1)} %collective-permute-done.6, ...), kind=kLoop, calls=%fused_computation.111 | loop fusion | flops 6003200 | bytes 9605190 | tf_op jit(solution)/shard_map/jit(_where)/select_n | solution.py:83
  305.1 111.4 %fusion.104 = bf16[128,64,128]{2,0,1:T(8,128)(2,1)} fusion(f32[134,70,128]{2,0,1:T(8,128)} %maximum_select_fusion, f32[128]{0:T(128)S(1)} %get-tuple-element.150, f32[128]{0:T(128)S(1)} %get-tuple-element.151, f32[128]{0:T(128)S(1)} %get-tuple-element.104, f32[128]{0:T(128)S(1)} %get-tuple-element.105, f32[128]{0:T(128)S(1)} %get-tuple-element.106, ...), kind=kLoop, calls=%fused_computation.210 | loop fusion | flops 104857600 | bytes 209740288 | tf_op jit(solution)/shard_map/convert_element_type | solution.py:140
  416.5 4.3 copy.27
  420.7 1.7 broadcast_multiply_fusion
  422.4 1.7 broadcast_multiply_fusion.1
  (60 shorter events, 0.4 us)
Async XLA Ops:
  7.2 57.6 %copy-start = (bf16[128,512]{1,0:T(8,128)(2,1)S(1)}, bf16[128,512]{1,0:T(8,128)(2,1)}, u32[]{:S(2)}) copy-start(bf16[128,512]{1,0:T(8,128)(2,1)} %param.17) | copy-start | bytes 393220
  7.2 10.7 %copy-start.6 = (f32[7,7,128]{2,1,0:T(8,128)S(1)}, f32[7,7,128]{2,1,0:T(8,128)}, u32[]{:S(2)}) copy-start(f32[7,7,128]{2,1,0:T(8,128)} %param.13) | copy-start | bytes 75268
  7.2 10.7 %copy-start.10 = (f32[128]{0:T(128)S(1)}, f32[128]{0:T(128)}, u32[]{:S(2)}) copy-start(f32[128]{0:T(128)} %param.21) | copy-start | bytes 1540
  7.2 292.3 %all-reduce.9.cloned.1.call-start = ((), (), s32[]{:S(2)}) async-start(), calls=%async_computation.1 | async-start | bytes 1048576 | tf_op jit(solution)/shard_map/psum | solution.py:143
  7.3 10.7 %copy-start.3 = (bf16[128,64,128]{2,1,0:T(8,128)(2,1)S(1)}, bf16[128,64,128]{2,1,0:T(8,128)(2,1)}, u32[]{:S(2)}) copy-start(bf16[128,64,128]{2,1,0:T(8,128)(2,1)} %param.12) | copy-start | bytes 6291460
  10.4 8.8 %collective-permute-start = (bf16[3,64,128]{2,0,1:T(4,128)(2,1)S(1)}, bf16[3,64,128]{2,0,1:T(4,128)(2,1)S(1)}, u32[]{:S(2)}, u32[]{:S(2)}) collective-permute-start(bf16[3,64,128]{2,0,1:T(4,128)(2,1)S(1)} %get-tuple-element.101), channel_id=1, source_target_pairs={{0,8},{8,16},{16,24},{24,32},{32,40},{40,48},{48,56},{56,64},{64,7... | collective-permute-start | bytes 147464 | tf_op jit(solution)/shard_map/ppermute | solution.py:17
  13.0 6.3 %collective-permute-start.1 = (bf16[3,64,128]{2,0,1:T(4,128)(2,1)S(1)}, bf16[3,64,128]{2,0,1:T(4,128)(2,1)S(1)}, u32[]{:S(2)}, u32[]{:S(2)}) collective-permute-start(bf16[3,64,128]{2,0,1:T(4,128)(2,1)S(1)} %get-tuple-element.102), channel_id=1, source_target_pairs={{8,0},{16,8},{24,16},{32,24},{40,32},{48,40},{56,48},{64,56},{72,6... | collective-permute-start | bytes 147464 | tf_op jit(solution)/shard_map/ppermute | solution.py:19
  19.1 9.9 %copy-start.11 = (f32[128]{0:T(128)S(1)}, f32[128]{0:T(128)}, u32[]{:S(2)}) copy-start(f32[128]{0:T(128)} %param.14) | copy-start | bytes 1540
  19.3 4.3 %collective-permute-start.2 = (bf16[134,3,128]{2,0,1:T(8,128)(2,1)S(1)}, bf16[134,3,128]{2,0,1:T(8,128)(2,1)S(1)}, u32[]{:S(2)}, u32[]{:S(2)}) collective-permute-start(bf16[134,3,128]{2,0,1:T(8,128)(2,1)S(1)} %get-tuple-element.99), channel_id=1, source_target_pairs={{0,1},{1,2},{2,3},{3,4},{4,5},{5,6},{6,7},{7,0},{8,9},{9,10},{10,1... | collective-permute-start | bytes 308744 | tf_op jit(solution)/shard_map/ppermute | solution.py:17
  21.9 4.1 collective-permute-start.3
  62.0 2.8 copy-start.7
  62.0 2.8 copy-start.8
  62.0 2.8 copy-start.9
  64.8 8.7 %copy-start.4 = (bf16[128,64,128]{2,1,0:T(8,128)(2,1)S(1)}, bf16[128,64,128]{2,1,0:T(8,128)(2,1)}, u32[]{:S(2)}) copy-start(bf16[128,64,128]{2,1,0:T(8,128)(2,1)} %param.12) | copy-start | bytes 6291460
  64.8 8.6 %copy-start.12 = (bf16[512,128]{1,0:T(8,128)(2,1)S(1)}, bf16[512,128]{1,0:T(8,128)(2,1)}, u32[]{:S(2)}) copy-start(bf16[512,128]{1,0:T(8,128)(2,1)} %param.19) | copy-start | bytes 393220
  93.3 32.8 %slice-start = ((s8[8388608]{0:T(1024)(128)(4,1)}), s8[4194304]{0:T(1024)(128)(4,1)S(1)}, s32[]{:S(2)}) async-start(s8[8388608]{0:T(1024)(128)(4,1)} %bitcast.185), calls=%async_computation.2 | async-start | bytes 8388608
  106.7 19.3 %copy-start.2 = (f32[128,64,128]{2,0,1:T(8,128)}, f32[128,64,128]{2,0,1:T(8,128)S(1)}, u32[]{:S(2)}) copy-start(f32[128,64,128]{2,0,1:T(8,128)S(1)} %get-tuple-element.92) | copy-start | bytes 12582916
  106.8 19.4 %slice-start.1 = ((s8[8388608]{0:T(1024)(128)(4,1)}), s8[4194304]{0:T(1024)(128)(4,1)S(1)}, s32[]{:S(2)}) async-start(s8[8388608]{0:T(1024)(128)(4,1)} %bitcast.185), calls=%async_computation.3 | async-start | bytes 8388608
  117.8 8.3 %copy-start.5 = (bf16[128,64,128]{2,1,0:T(8,128)(2,1)S(1)}, bf16[128,64,128]{2,1,0:T(8,128)(2,1)}, u32[]{:S(2)}) copy-start(bf16[128,64,128]{2,1,0:T(8,128)(2,1)} %param.12) | copy-start | bytes 6291460
  126.2 4.4 %copy-start.13 = (f32[128]{0:T(128)S(1)}, f32[128]{0:T(128)}, u32[]{:S(2)}) copy-start(f32[128]{0:T(128)} %param.20) | copy-start | bytes 1540
  224.4 7.2 %collective-permute-start.4 = (f32[3,64,128]{2,0,1:T(4,128)S(1)}, f32[3,64,128]{2,0,1:T(4,128)S(1)}, u32[]{:S(2)}, u32[]{:S(2)}) collective-permute-start(f32[3,64,128]{2,0,1:T(4,128)S(1)} %get-tuple-element.97), channel_id=1, source_target_pairs={{0,8},{8,16},{16,24},{24,32},{32,40},{40,48},{48,56},{56,64},{64,7... | collective-permute-start | bytes 294920 | tf_op jit(solution)/shard_map/ppermute | solution.py:17
  224.4 7.2 %collective-permute-start.5 = (f32[3,64,128]{2,0,1:T(4,128)S(1)}, f32[3,64,128]{2,0,1:T(4,128)S(1)}, u32[]{:S(2)}, u32[]{:S(2)}) collective-permute-start(f32[3,64,128]{2,0,1:T(4,128)S(1)} %get-tuple-element.98), channel_id=1, source_target_pairs={{8,0},{16,8},{24,16},{32,24},{40,32},{48,40},{56,48},{64,56},{72,6... | collective-permute-start | bytes 294920 | tf_op jit(solution)/shard_map/ppermute | solution.py:19
  229.7 191.0 %all-reduce.7.cloned.1.call-start = ((), (), s32[]{:S(2)}) async-start(), calls=%async_computation | async-start | bytes 1048576 | tf_op jit(solution)/shard_map/psum | solution.py:142
  232.6 66.9 %collective-permute-start.6 = (f32[134,3,128]{2,0,1:T(8,128)S(1)}, f32[134,3,128]{2,0,1:T(8,128)S(1)}, u32[]{:S(2)}, u32[]{:S(2)}) collective-permute-start(f32[134,3,128]{2,0,1:T(8,128)S(1)} %get-tuple-element.95), channel_id=1, source_target_pairs={{0,1},{1,2},{2,3},{3,4},{4,5},{5,6},{6,7},{7,0},{8,9},{9,10},{10,1... | collective-permute-start | bytes 617480 | tf_op jit(solution)/shard_map/ppermute | solution.py:17
  249.3 50.3 %collective-permute-start.7 = (f32[134,3,128]{2,0,1:T(8,128)S(1)}, f32[134,3,128]{2,0,1:T(8,128)S(1)}, u32[]{:S(2)}, u32[]{:S(2)}) collective-permute-start(f32[134,3,128]{2,0,1:T(8,128)S(1)} %get-tuple-element.96), channel_id=1, source_target_pairs={{1,0},{2,1},{3,2},{4,3},{5,4},{6,5},{7,6},{0,7},{9,8},{10,9},{11,1... | collective-permute-start | bytes 617480 | tf_op jit(solution)/shard_map/ppermute | solution.py:19
  305.1 119.0 %copy-start.1 = (bf16[128,512]{1,0:T(8,128)(2,1)S(1)}, bf16[128,512]{1,0:T(8,128)(2,1)}, u32[]{:S(2)}) copy-start(bf16[128,512]{1,0:T(8,128)(2,1)} %param.17) | copy-start | bytes 393220
Sparse Core Ops, SparseCore 0:
  229.8 69.6 all-reduce.8
  302.8 85.7 all-reduce.6
